TPU v7x, 128 devices: a whole 4x4x4 slice. The times are simulated.
128 devices in a mesh: ctx: 32 (over z, x, core), exp: 4 (over y).
Axes of the slice: x: 4, y: 4, z: 4, core: 2. Of those that a mesh axis runs over, the one named last changes fastest.
Arguments:
- queries: bfloat16 [16384, 6144], P('ctx', 'exp'), may hold values from -0.52734375 to 0.52734375
- key_vectors: bfloat16 [16384, 6144], P('ctx', 'exp'), may hold values from -6 to 6
- values: bfloat16 [16384, 6144], P('ctx', 'exp'), may hold values from -6 to 6
- log_decay: float32 [16384, 48], P('ctx', 'exp'), may hold values from -1 to 0, as said below
- out_gate: bfloat16 [16384, 6144], P(('ctx', 'exp')), may hold values from -6 to 6
- residual: bfloat16 [16384, 6144], P(('ctx', 'exp')), may hold values from -6 to 6
- attn_gain: float32 [6144], replicated, may hold values from 0.1 to 1.9
- moe_gain: float32 [6144], replicated, may hold values from 0.1 to 1.9
- expert_ids: int32 [16384, 2], P(('ctx', 'exp')), may hold values from 0 to 31, as said below
- route_weights: float32 [16384, 2], P(('ctx', 'exp')), may hold values from 0.5 to 1.5
- w_gate: bfloat16 [4, 6144, 9216], P('exp', None, 'ctx'), may hold values from -0.078125 to 0.078125
- w_up: bfloat16 [4, 6144, 9216], P('exp', None, 'ctx'), may hold values from -0.078125 to 0.078125
- w_down: bfloat16 [4, 9216, 6144], P('exp', 'ctx'), may hold values from -0.0625 to 0.0625
Outputs:
- hidden: bfloat16 [16384, 6144], P(('ctx', 'exp'))
- moe_out: bfloat16 [16384, 6144], P(('ctx', 'exp'))
Inputs may be any that keep to these rules, and one draw needn't show every extreme that they name: `expert_ids`: each token names two different experts, at most one of them below 4. The 128 rows of one device name each expert below 4 at most 4 times; in every draw one expert is named exactly 4 times by every device of some index of ctx. `log_decay`: every entry is negative.
All inputs are finite; a program needn't handle non-finite values.
Results may differ from a plain program's by a relative error of at most 0.03.
Values may be sent and summed in bfloat16 or wider, within the bound.
No kernel may reach another device: no remote copies, remote signals or barrier semaphores. Data moves between devices by JAX's collectives and lax.ppermute only.
A program may use at most 128 MiB of HBM per device.

v0:
```python
import jax
import jax.numpy as jnp
from jax import lax
from jax.sharding import PartitionSpec as P

HEAD_DIM = 128
CAP = 4


def entering(shard, axis, combine, identity):
    peers, place = (lax.axis_size(axis), lax.axis_index(axis))
    everything = jax.tree.map(
        lambda part, kind: lax.all_gather(part.astype(kind), axis),
        shard,
        (jnp.bfloat16, jnp.bfloat16),
    )
    start = jax.tree.map(
        lambda part, zero: jnp.broadcast_to(jnp.asarray(zero, part.dtype), part.shape),
        shard,
        identity,
    )

    def turn(k, before):
        reached = k < place
        new = combine(
            before, jax.tree.map(lambda part, own: part[k].astype(own.dtype), everything, shard)
        )
        return jax.tree.map(lambda a, b: jnp.where(reached, a, b), new, before)

    return lax.fori_loop(0, peers, turn, start)


def combine_states(earlier, later):
    return (earlier[0] * later[0], later[0][:, None, None] * earlier[1] + later[1])


def local(
    queries,
    key_vectors,
    values,
    log_decay,
    out_gate,
    residual,
    attn_gain,
    moe_gain,
    expert_ids,
    route_weights,
    w_gate,
    w_up,
    w_down,
):
    highest = lax.Precision.HIGHEST
    row_total = queries.shape[0]
    head_count = log_decay.shape[1]
    query_heads = queries.reshape(row_total, head_count, HEAD_DIM)
    key_heads = key_vectors.reshape(row_total, head_count, HEAD_DIM)
    value_heads = values.reshape(row_total, head_count, HEAD_DIM)
    cumulative = jnp.cumsum(log_decay, axis=0)
    final_cum = cumulative[-1]
    weighted_keys = (
        key_heads.astype(jnp.float32) * jnp.exp(final_cum[None, :] - cumulative)[:, :, None]
    )
    local_state = jnp.einsum(
        "shd,she->hde", weighted_keys, value_heads.astype(jnp.float32), precision=highest
    )
    block_decay = jnp.exp(final_cum)
    prior = entering(
        (block_decay, local_state),
        "ctx",
        combine_states,
        (jnp.ones_like(block_decay), jnp.zeros_like(local_state)),
    )
    carried = prior[1]
    block_size = min(512, row_total)

    def query_part(block_index):
        offset = block_index * block_size
        scores = jnp.einsum(
            "thd,shd->hts", query_heads, key_heads, preferred_element_type=jnp.float32
        )
        log_gap = cumulative.T[:, :, None] - cumulative.T[:, None, :]
        causal = (offset + jnp.arange(block_size))[:, None] >= jnp.arange(row_total)[None, :]
        decay_now = jnp.where(causal[None], jnp.exp(jnp.minimum(log_gap, 0.0)), 0.0)
        weights = (scores * decay_now).astype(jnp.bfloat16)
        inside = jnp.einsum(
            "hts,shd->thd", weights, value_heads, preferred_element_type=jnp.float32
        )
        scaled = query_heads.astype(jnp.float32) * jnp.exp(cumulative)[:, :, None]
        carried_part = jnp.einsum("thd,hde->the", scaled, carried, precision=highest)
        return (inside + carried_part).astype(jnp.bfloat16)

    blocks_out = lax.map(query_part, jnp.arange(row_total // block_size))
    attention = blocks_out.reshape(row_total, head_count * HEAD_DIM)
    token_rows = lax.all_to_all(attention, "exp", split_axis=0, concat_axis=1, tiled=True)
    attn_f32 = token_rows.astype(jnp.float32)
    attn_norm = (
        attn_f32
        * lax.rsqrt(jnp.mean(attn_f32 * attn_f32, axis=-1, keepdims=True) + 1e-05)
        * attn_gain
    )
    hidden = (
        residual.astype(jnp.float32) + attn_norm * jax.nn.sigmoid(out_gate.astype(jnp.float32))
    ).astype(jnp.bfloat16)
    hidden_f32 = hidden.astype(jnp.float32)
    normed = (
        hidden_f32
        * lax.rsqrt(jnp.mean(hidden_f32 * hidden_f32, axis=-1, keepdims=True) + 1e-05)
        * moe_gain
    ).astype(jnp.bfloat16)
    held_count = lax.axis_size("exp")
    expert_index = jnp.arange(held_count, dtype=jnp.int32)
    naming = expert_ids[:, :, None] == expert_index[None, None, :]
    member = jnp.any(naming, axis=1)
    slot_rank = jnp.cumsum(member.astype(jnp.int32), axis=0) - 1
    slot_index = jnp.arange(CAP, dtype=jnp.int32)
    placing = (
        member.T[:, None, :] & (slot_rank.T[:, None, :] == slot_index[None, :, None])
    ).astype(jnp.bfloat16)
    outgoing = jnp.einsum(
        "jct,td->jcd", placing, normed, preferred_element_type=jnp.float32
    ).astype(jnp.bfloat16)
    incoming = lax.all_to_all(outgoing, "exp", split_axis=0, concat_axis=0, tiled=True)
    flat_rows = incoming.reshape(held_count * CAP, incoming.shape[2])
    gate_matrix = w_gate[0]
    up_matrix = w_up[0]
    down_matrix = w_down[0]
    pieces = lax.all_gather(flat_rows, "ctx", axis=0, tiled=True)
    gate_part = jnp.dot(pieces, gate_matrix, preferred_element_type=jnp.float32)
    up_part = jnp.dot(pieces, up_matrix, preferred_element_type=jnp.float32)
    activations = (jax.nn.silu(gate_part) * up_part).astype(jnp.bfloat16)
    summed = lax.psum_scatter(
        jnp.dot(activations, down_matrix, preferred_element_type=jnp.float32).astype(jnp.bfloat16),
        "ctx",
        scatter_dimension=0,
        tiled=True,
    ).astype(jnp.float32)
    leaving = summed.astype(jnp.bfloat16).reshape(held_count, CAP, summed.shape[1])
    returned = lax.all_to_all(leaving, "exp", split_axis=0, concat_axis=0, tiled=True)
    chosen = jnp.sum(jnp.where(expert_ids < held_count, route_weights, 0.0), axis=1)
    gathered_back = jnp.einsum("jct,jcd->td", placing, returned, preferred_element_type=jnp.float32)
    moe_out = (gathered_back * chosen[:, None]).astype(jnp.bfloat16)
    return (hidden, moe_out)


def solution(mesh):
    in_specs = (
        P("ctx", "exp"),
        P("ctx", "exp"),
        P("ctx", "exp"),
        P("ctx", "exp"),
        P(("ctx", "exp"), None),
        P(("ctx", "exp"), None),
        P(),
        P(),
        P(("ctx", "exp"), None),
        P(("ctx", "exp"), None),
        P("exp", None, "ctx"),
        P("exp", None, "ctx"),
        P("exp", "ctx", None),
    )
    out_specs = (P(("ctx", "exp"), None), P(("ctx", "exp"), None))
    return jax.shard_map(local, mesh=mesh, in_specs=in_specs, out_specs=out_specs, check_vma=False)
```

profile of v0, /device:TPU:0, one launch (start us, length us, event | category | flops | bytes accessed | tf_op | source)
XLA Modules:
  0.0 408.7 jit_solution(17558675305011067984)
XLA Ops:
  10.1 3.1 reduce-window.6
  15.9 2.6 copy.101
  18.5 2.6 copy.106
  22.4 4.3 %fusion.35 = bf16[12,128,128]{2,1,0:T(8,128)(2,1)} fusion(bf16[512,12,128]{0,2,1:T(8,128)(2,1)} %bitcast.85, bf16[512,12,128]{0,2,1:T(8,128)(2,1)} %bitcast.83, f32[512,12]{0,1:T(8,128)S(1)} %get-tuple-element.175), kind=kOutput, calls=%fused_computation.42 | convolution fusion | flops 1209729024 | bytes 3563520 | tf_op jit(solution)/shard_map/shd,she->hde/dot_general | solution.py:63
  27.7 22.8 %all-gather.1 = bf16[32,1,12]{2,1,0:T(2,128)(2,1)S(1)} all-gather(bf16[1,1,12]{2,1,0:T(2,128)(2,1)S(1)} %bitcast.98), channel_id=1, replica_groups=mesh['ctx'=32,'exp'=4] {'ctx'}, dimensions={0}, use_global_device_ids=true | all-gather | bytes 792 | tf_op jit(solution)/shard_map/all_gather | solution.py:13
  50.5 2.6 copy.100
  53.9 38.4 %all-gather.7.cloned.1.call-done = bf16[384,128,128]{2,1,0:T(8,128)(2,1)} async-done(((bf16[12,128,128]{2,1,0:T(8,128)(2,1)}), bf16[384,128,128]{2,1,0:T(8,128)(2,1)}) %all-gather.7.cloned.1.call-update) | async-done | bytes 12582928 | tf_op jit(solution)/shard_map/all_gather | solution.py:13
  92.4 72.8 %while.18 = (s32[]{:T(128)}, f32[12,128,128]{2,1,0:T(8,128)}, s32[]{:T(128)}, bf16[32,12]{1,0:T(8,128)(2,1)S(1)}, bf16[32,12,128,128]{3,2,1,0:T(8,128)(2,1)}, /*index=5*/s32[]{:T(128)}, s32[]{:T(128)}) while((s32[]{:T(128)}, f32[12,128,128]{2,1,0:T(8,128)}, s32[]{:T(128)}, bf16[32,12]{1,0:T(8,128)(2,1)S(1)}, ...), condition=%wide.region_3.4_spmd.clone, body=%wide.region_2.3_spmd.clone.sunk | while | flops 983056 | bytes 1966305 | solution.py:30
  99.0 2.3 fusion.61
  101.3 2.3 fusion.61
  105.8 2.3 fusion.61
  108.1 2.3 fusion.61
  114.9 2.3 fusion.61
  165.1 8.3 %fusion.20 = f32[12,128,512]{1,2,0:T(8,128)} fusion(f32[12,128,128]{2,1,0:T(8,128)} %get-tuple-element.117, bf16[512,12,128]{0,2,1:T(8,128)(2,1)} %bitcast.87, f32[512,12]{0,1:T(8,128)} %get-tuple-element.174), kind=kOutput, calls=%fused_computation.30 | convolution fusion | flops 1209532416 | bytes 5529600 | tf_op jit(solution)/shard_map/while/body/eval_jaxpr/thd,hde->the/dot_general | solution.py:89
  173.4 8.8 %fusion.19 = bf16[512,12,128]{2,0,1:T(8,128)(2,1)} fusion(f32[12,128,512]{1,2,0:T(8,128)} %fusion.20, bf16[512,12,128]{0,2,1:T(8,128)(2,1)} %bitcast.86, f32[12,512]{1,0:T(8,128)} %bitcast.93, pred[512,512]{1,0:T(8,128)(4,1)} %iota_compare_fusion, bf16[512,12,128]{0,2,1:T(8,128)(2,1)} %bitcast.88, bf16[512,12,128]{0,2,1:T(8,128)(2,1)} %bitcast.84), kind=kOutput, calls=%fused_computation.28 | convolution fusion | flops 1627914240 | bytes 9723904 | tf_op jit(solution)/shard_map/while/body/eval_jaxpr/hts,shd->thd/dot_general | solution.py:85
  182.2 2.6 copy.114
  184.8 3.5 all_to_all.16
  188.3 2.8 copy.115
  191.1 4.3 %all-to-all-start = ((bf16[4,128,1536]{1,2,0:T(8,128)(2,1)}), bf16[4,128,1536]{1,2,0:T(8,128)(2,1)}, u32[]{:S(2)}, u32[]{:S(2)}) async-start(bf16[4,128,1536]{1,2,0:T(8,128)(2,1)} %copy.115), calls=%async_computation | async-start | bytes 3145728 | tf_op jit(solution)/shard_map/all_to_all | solution.py:94
  195.7 2.6 copy.116
  198.2 2.6 copy.99
  205.6 11.3 %all-to-all-done = bf16[4,128,1536]{1,2,0:T(8,128)(2,1)} async-done(((bf16[4,128,1536]{1,2,0:T(8,128)(2,1)}), bf16[4,128,1536]{1,2,0:T(8,128)(2,1)}, u32[]{:S(2)}, u32[]{:S(2)}) %all-to-all-start) | async-done | bytes 1572896 | tf_op jit(solution)/shard_map/all_to_all | solution.py:94
  219.1 3.2 fusion.12
  224.7 9.4 %all_to_all.23 = bf16[4,4,6144]{2,1,0:T(4,128)(2,1)} all-to-all(bf16[4,4,6144]{2,1,0:T(4,128)(2,1)S(1)} %convolution_convert_fusion.1), channel_id=1, replica_groups=mesh['ctx'=32,'exp'=4] {'exp'}, dimensions={0} | all-to-all | bytes 393216 | tf_op jit(solution)/shard_map/all_to_all | solution.py:122
  235.8 47.0 %all-gather.5.cloned.1.call-done = bf16[512,6144]{1,0:T(8,128)(2,1)} async-done(((bf16[16,6144]{1,0:T(8,128)(2,1)}), bf16[512,6144]{1,0:T(8,128)(2,1)}) %all-gather.5.cloned.1.call-update) | async-done | bytes 6291472 | tf_op jit(solution)/shard_map/all_gather | solution.py:127
  282.7 6.7 %fusion.10 = f32[512,288]{0,1:T(8,128)} fusion(bf16[512,6144]{1,0:T(8,128)(2,1)} %all-gather.5.cloned.1.call-done, bf16[1,6144,288]{1,2,0:T(8,128)(2,1)} %param.25), kind=kOutput, calls=%fused_computation.17 | convolution fusion | flops 1811939328 | bytes 10420224 | tf_op jit(solution)/shard_map/dot_general | solution.py:128
  289.4 12.1 %convolution_convert_fusion = bf16[512,6144]{1,0:T(8,128)(2,1)} fusion(bf16[1,288,6144]{2,1,0:T(8,128)(2,1)S(1)} %copy-done, bf16[512,6144]{1,0:T(8,128)(2,1)} %all-gather.5.cloned.1.call-done, bf16[1,6144,288]{1,2,0:T(8,128)(2,1)} %param.26, f32[512,288]{0,1:T(8,128)} %fusion.10), kind=kOutput, calls=%fused_computation.4 | convolution fusion | flops 3627909120 | bytes 20250624 | tf_op jit(solution)/shard_map/dot_general | solution.py:132
  301.5 85.5 %reduce-scatter.2.cloned.1.call-done = bf16[16,6144]{1,0:T(8,128)(2,1)} async-done(((bf16[512,6144]{1,0:T(8,128)(2,1)}), bf16[16,6144]{1,0:T(8,128)(2,1)}) %reduce-scatter.2.cloned.1.call-update) | async-done | bytes 196624 | tf_op jit(solution)/shard_map/reduce_scatter | solution.py:131
  388.6 4.3 %all-to-all-start.2 = ((bf16[4,4,6144]{2,1,0:T(4,128)(2,1)}), bf16[4,4,6144]{2,1,0:T(4,128)(2,1)}, u32[]{:S(2)}, u32[]{:S(2)}) async-start(bf16[4,4,6144]{2,1,0:T(4,128)(2,1)} %reshape.116), calls=%async_computation.3 | async-start | bytes 393216 | tf_op jit(solution)/shard_map/all_to_all | solution.py:138
  392.9 2.6 copy.122
  395.5 3.8 all-to-all-done.2
  399.3 2.8 fusion.2
  (106 shorter events, 82.9 us)
Async XLA Ops:
  7.2 282.2 %copy-start = (bf16[1,288,6144]{2,1,0:T(8,128)(2,1)S(1)}, bf16[1,288,6144]{2,1,0:T(8,128)(2,1)}, u32[]{:S(2)}) copy-start(bf16[1,288,6144]{2,1,0:T(8,128)(2,1)} %param.27) | copy-start | bytes 10616836
  7.2 85.2 %all-gather.7.cloned.1.call-start = ((), (), s32[]{:S(2)}) async-start(), calls=%async_computation.6 | async-start | bytes 12976128 | tf_op jit(solution)/shard_map/all_gather | solution.py:13
  15.1 0.6 copy-start.2
  191.1 25.8 %all-to-all-start = ((bf16[4,128,1536]{1,2,0:T(8,128)(2,1)}), bf16[4,128,1536]{1,2,0:T(8,128)(2,1)}, u32[]{:S(2)}, u32[]{:S(2)}) async-start(bf16[4,128,1536]{1,2,0:T(8,128)(2,1)} %copy.115), calls=%async_computation | async-start | bytes 3145728 | tf_op jit(solution)/shard_map/all_to_all | solution.py:94
  195.4 5.4 %copy-start.3 = (s32[128,2]{0,1:T(2,128)S(1)}, s32[128,2]{0,1:T(2,128)}, u32[]{:S(2)}) copy-start(s32[128,2]{0,1:T(2,128)} %param.23) | copy-start | bytes 3076
  195.4 87.3 %all-gather.5.cloned.1.call-start = ((), (), s32[]{:S(2)}) async-start(), calls=%async_computation.4 | async-start | bytes 6488064 | tf_op jit(solution)/shard_map/all_gather | solution.py:127
  219.1 4.3 %copy-start.5 = (f32[6144]{0:T(1024)S(1)}, f32[6144]{0:T(1024)}, u32[]{:S(2)}) copy-start(f32[6144]{0:T(1024)} %param.22) | copy-start | bytes 73732
  222.3 1.1 copy-start.1
  235.7 151.2 %reduce-scatter.2.cloned.1.call-start = ((), (), s32[]{:S(2)}) async-start(), calls=%async_computation.5 | async-start | bytes 6488064 | tf_op jit(solution)/shard_map/reduce_scatter | solution.py:131
  301.5 91.4 %copy-start.4 = (f32[128,2]{0,1:T(2,128)S(1)}, f32[128,2]{0,1:T(2,128)}, u32[]{:S(2)}) copy-start(f32[128,2]{0,1:T(2,128)} %param.24) | copy-start | bytes 3076
  388.6 10.7 %all-to-all-start.2 = ((bf16[4,4,6144]{2,1,0:T(4,128)(2,1)}), bf16[4,4,6144]{2,1,0:T(4,128)(2,1)}, u32[]{:S(2)}, u32[]{:S(2)}) async-start(bf16[4,4,6144]{2,1,0:T(4,128)(2,1)} %reshape.116), calls=%async_computation.3 | async-start | bytes 393216 | tf_op jit(solution)/shard_map/all_to_all | solution.py:138
Sparse Core Ops, SparseCore 0:
  26.9 65.4 all-gather.6
  235.8 46.8 all-gather.4
  301.6 85.2 reduce-scatter.1
where the time goes:
time: 411 us; the launch traced here: 409 us
  waiting for transfers between devices  186 us (45%)
  other arithmetic  88.4 us (22%)
  matrix products  44.2 us (11%)
  local copies, waits for them, and re-layouts  35.1 us (9%)
  blocking collectives  32.2 us (8%)
  between operations  13.9 us (3%)
  starting transfers between devices  8.89 us (2%)
    reduce_scatter x1, waiting for transfers between devices, local(): lax.psum_scatter(jnp.dot(activations, down_matrix, preferred_element_type...  85.5 us
    select_n x32, other arithmetic, turn(): return jax.tree.map(lambda a, b: jnp.where(reached, a, b), new, before)  72.5 us
    all_gather x1, waiting for transfers between devices, local(): pieces = lax.all_gather(flat_rows, 'ctx', axis=0, tiled=True)  47 us
    all_gather x1, waiting for transfers between devices, entering(): lax.all_gather(part.astype(kind), axis)  38.4 us
    all_gather x1, blocking collectives, entering(): lax.all_gather(part.astype(kind), axis)  22.8 us
    unnamed x21, local copies, waits for them, and re-layouts  17.3 us
    dot_general x1, matrix products, local(): jnp.dot(activations, down_matrix, preferred_element_type=jnp.float32)  12.1 us
    all_to_all x1, waiting for transfers between devices, local(): lax.all_to_all(attention, 'exp', split_axis=0, concat_axis=1, tiled=True)  11.3 us
  transfers between devices with their start and end apart: 5, of which 5 were waited for; matrix products, arithmetic and copies ran while one was open for 4% of the time, Pallas kernels for 0%

commit v1 on v0

--- a/solution.py
+++ b/solution.py
@@ -124,7 +124,9 @@
     gate_matrix = w_gate[0]
     up_matrix = w_up[0]
     down_matrix = w_down[0]
-    pieces = lax.all_gather(flat_rows, "ctx", axis=0, tiled=True)
+    pieces = jnp.concatenate(
+        lax.all_to_all(jnp.stack([flat_rows] * lax.axis_size("ctx")), "ctx", 0, 0), axis=0
+    )
     gate_part = jnp.dot(pieces, gate_matrix, preferred_element_type=jnp.float32)
     up_part = jnp.dot(pieces, up_matrix, preferred_element_type=jnp.float32)
     activations = (jax.nn.silu(gate_part) * up_part).astype(jnp.bfloat16)

time: 411 us -> 441 us (1.073)
  blocking collectives: 32.2 us -> 111 us
  waiting for transfers between devices: 186 us -> 137 us
    all_to_all x0 -> x1, blocking collectives: none -> 79 us  [local(): lax.all_to_all(jnp.stack([flat_rows] * lax.axis_size('ctx')), 'ctx', 0, 0)]
    all_gather x1 -> x0, waiting for transfers between devices: 47 us -> none  [local(): pieces = lax.all_gather(flat_rows, 'ctx', axis=0, tiled=True)]
    unnamed x21 -> x25, local copies, waits for them, and re-layouts: 17.3 us -> 19.9 us
  transfers between devices with their start and end apart: 5 -> 4, of which waited for: 5 -> 4; matrix products, arithmetic and copies ran while one was open for 4% -> 4% of each run, Pallas kernels for 0% -> 0%
where the time goes in v1:
time: 441 us; the launch traced here: 439 us
  waiting for transfers between devices  137 us (31%)
  blocking collectives  111 us (25%)
  other arithmetic  88.4 us (20%)
  matrix products  40.3 us (9%)
  local copies, waits for them, and re-layouts  39.4 us (9%)
  between operations  14.2 us (3%)
  starting transfers between devices  8.88 us (2%)
    reduce_scatter x1, waiting for transfers between devices, local(): lax.psum_scatter(jnp.dot(activations, down_matrix, preferred_element_type...  83.3 us
    all_to_all x1, blocking collectives, local(): lax.all_to_all(jnp.stack([flat_rows] * lax.axis_size('ctx')), 'ctx', 0, 0)  79 us
    select_n x32, other arithmetic, turn(): return jax.tree.map(lambda a, b: jnp.where(reached, a, b), new, before)  72.5 us
    all_gather x1, waiting for transfers between devices, entering(): lax.all_gather(part.astype(kind), axis)  38.4 us
    all_gather x1, blocking collectives, entering(): lax.all_gather(part.astype(kind), axis)  22.8 us
    unnamed x25, local copies, waits for them, and re-layouts  19.9 us
    dot_general x1, matrix products, local(): jnp.dot(activations, down_matrix, preferred_element_type=jnp.float32)  12.1 us
    all_to_all x1, waiting for transfers between devices, local(): lax.all_to_all(attention, 'exp', split_axis=0, concat_axis=1, tiled=True)  11.3 us
  transfers between devices with their start and end apart: 4, of which 4 were waited for; matrix products, arithmetic and copies ran while one was open for 4% of the time, Pallas kernels for 0%

profile of v1, /device:TPU:0, one launch (start us, length us, event | category | flops | bytes accessed | tf_op | source)
XLA Modules:
  0.0 439.3 jit_solution(16828029567589078754)
XLA Ops:
  10.1 3.1 reduce-window.6
  15.9 2.6 copy.101
  18.5 2.6 copy.106
  22.4 4.3 fusion.35
  27.7 22.8 %all-gather.1 = bf16[32,1,12]{2,1,0:T(2,128)(2,1)S(1)} all-gather(bf16[1,1,12]{2,1,0:T(2,128)(2,1)S(1)} %bitcast.101), channel_id=1, replica_groups=mesh['ctx'=32,'exp'=4] {'ctx'}, dimensions={0}, use_global_device_ids=true | all-gather | bytes 792 | tf_op jit(solution)/shard_map/all_gather | solution.py:13
  50.5 2.6 copy.100
  53.9 38.4 %all-gather.4.cloned.1.call-done = bf16[384,128,128]{2,1,0:T(8,128)(2,1)} async-done(((bf16[12,128,128]{2,1,0:T(8,128)(2,1)}), bf16[384,128,128]{2,1,0:T(8,128)(2,1)}) %all-gather.4.cloned.1.call-update) | async-done | bytes 12582928 | tf_op jit(solution)/shard_map/all_gather | solution.py:13
  92.4 72.8 %while.18 = (s32[]{:T(128)}, f32[12,128,128]{2,1,0:T(8,128)}, s32[]{:T(128)}, bf16[32,12]{1,0:T(8,128)(2,1)S(1)}, bf16[32,12,128,128]{3,2,1,0:T(8,128)(2,1)}, /*index=5*/s32[]{:T(128)}, s32[]{:T(128)}) while((s32[]{:T(128)}, f32[12,128,128]{2,1,0:T(8,128)}, s32[]{:T(128)}, bf16[32,12]{1,0:T(8,128)(2,1)S(1)}, ...), condition=%wide.region_3.4_spmd.clone, body=%wide.region_2.3_spmd.clone.sunk | while | flops 983056 | bytes 1966305 | solution.py:30
  99.0 2.3 fusion.61
  101.3 2.3 fusion.61
  105.8 2.3 fusion.61
  108.1 2.3 fusion.61
  165.1 8.3 %fusion.20 = f32[12,128,512]{1,2,0:T(8,128)} fusion(f32[12,128,128]{2,1,0:T(8,128)} %get-tuple-element.117, bf16[512,12,128]{0,2,1:T(8,128)(2,1)} %bitcast.90, f32[512,12]{0,1:T(8,128)} %get-tuple-element.174), kind=kOutput, calls=%fused_computation.30 | convolution fusion | flops 1209532416 | bytes 5529600 | tf_op jit(solution)/shard_map/while/body/eval_jaxpr/thd,hde->the/dot_general | solution.py:89
  173.4 8.8 %fusion.19 = bf16[512,12,128]{2,0,1:T(8,128)(2,1)} fusion(f32[12,128,512]{1,2,0:T(8,128)} %fusion.20, bf16[512,12,128]{0,2,1:T(8,128)(2,1)} %bitcast.89, f32[12,512]{1,0:T(8,128)} %bitcast.96, pred[512,512]{1,0:T(8,128)(4,1)} %iota_compare_fusion, bf16[512,12,128]{0,2,1:T(8,128)(2,1)} %bitcast.91, bf16[512,12,128]{0,2,1:T(8,128)(2,1)} %bitcast.87), kind=kOutput, calls=%fused_computation.28 | convolution fusion | flops 1627914240 | bytes 9723904 | tf_op jit(solution)/shard_map/while/body/eval_jaxpr/hts,shd->thd/dot_general | solution.py:85
  182.2 2.6 copy.114
  184.8 3.5 all_to_all.19
  188.3 2.8 copy.115
  191.1 4.3 all-to-all-start
  195.7 2.6 copy.116
  198.2 2.6 copy.99
  205.6 11.3 %all-to-all-done = bf16[4,128,1536]{1,2,0:T(8,128)(2,1)} async-done(((bf16[4,128,1536]{1,2,0:T(8,128)(2,1)}), bf16[4,128,1536]{1,2,0:T(8,128)(2,1)}, u32[]{:S(2)}, u32[]{:S(2)}) %all-to-all-start) | async-done | bytes 1572896 | tf_op jit(solution)/shard_map/all_to_all | solution.py:94
  219.1 3.2 fusion.12
  224.7 9.4 %all_to_all.28 = bf16[4,4,6144]{2,1,0:T(4,128)(2,1)} all-to-all(bf16[4,4,6144]{2,1,0:T(4,128)(2,1)S(1)} %convolution_convert_fusion.1), channel_id=1, replica_groups=mesh['ctx'=32,'exp'=4] {'exp'}, dimensions={0} | all-to-all | bytes 393216 | tf_op jit(solution)/shard_map/all_to_all | solution.py:122
  237.4 79.0 %all_to_all.29 = bf16[32,16,6144]{2,1,0:T(8,128)(2,1)S(1)} all-to-all(bf16[32,16,6144]{2,1,0:T(8,128)(2,1)S(1)} %stack.3), channel_id=1, replica_groups=mesh['ctx'=32,'exp'=4] {'ctx'}, dimensions={0} | all-to-all | bytes 12582912 | tf_op jit(solution)/shard_map/all_to_all | solution.py:128
  316.4 2.7 copy-done.1
  319.0 2.8 fusion.10
  321.9 12.1 %convolution_convert_fusion = bf16[512,6144]{1,0:T(8,128)(2,1)} fusion(bf16[1,288,6144]{2,1,0:T(8,128)(2,1)S(1)} %copy-done, bf16[512,6144]{1,0:T(8,128)(2,1)} %bitcast.85, bf16[1,6144,288]{1,2,0:T(8,128)(2,1)} %param.26, f32[512,288]{0,1:T(8,128)} %fusion.10), kind=kOutput, calls=%fused_computation.4 | convolution fusion | flops 3627909120 | bytes 20250624 | tf_op jit(solution)/shard_map/dot_general | solution.py:134
  334.0 83.3 %reduce-scatter.2.cloned.1.call-done = bf16[16,6144]{1,0:T(8,128)(2,1)} async-done(((bf16[512,6144]{1,0:T(8,128)(2,1)}), bf16[16,6144]{1,0:T(8,128)(2,1)}) %reduce-scatter.2.cloned.1.call-update) | async-done | bytes 196624 | tf_op jit(solution)/shard_map/reduce_scatter | solution.py:133
  418.9 4.3 all-to-all-start.3
  423.2 2.6 copy.122
  425.8 3.8 all-to-all-done.3
  429.6 2.8 fusion.2
  (109 shorter events, 86.8 us)
Async XLA Ops:
  7.2 314.7 %copy-start = (bf16[1,288,6144]{2,1,0:T(8,128)(2,1)S(1)}, bf16[1,288,6144]{2,1,0:T(8,128)(2,1)}, u32[]{:S(2)}) copy-start(bf16[1,288,6144]{2,1,0:T(8,128)(2,1)} %param.27) | copy-start | bytes 10616836
  7.2 85.2 %all-gather.4.cloned.1.call-start = ((), (), s32[]{:S(2)}) async-start(), calls=%async_computation.6 | async-start | bytes 12976128 | tf_op jit(solution)/shard_map/all_gather | solution.py:13
  15.1 0.6 copy-start.3
  191.1 25.8 %all-to-all-start = ((bf16[4,128,1536]{1,2,0:T(8,128)(2,1)}), bf16[4,128,1536]{1,2,0:T(8,128)(2,1)}, u32[]{:S(2)}, u32[]{:S(2)}) async-start(bf16[4,128,1536]{1,2,0:T(8,128)(2,1)} %copy.115), calls=%async_computation | async-start | bytes 3145728 | tf_op jit(solution)/shard_map/all_to_all | solution.py:94
  195.4 5.4 %copy-start.4 = (s32[128,2]{0,1:T(2,128)S(1)}, s32[128,2]{0,1:T(2,128)}, u32[]{:S(2)}) copy-start(s32[128,2]{0,1:T(2,128)} %param.23) | copy-start | bytes 3076
  195.4 221.8 %reduce-scatter.2.cloned.1.call-start = ((), (), s32[]{:S(2)}) async-start(), calls=%async_computation.5 | async-start | bytes 6488064 | tf_op jit(solution)/shard_map/reduce_scatter | solution.py:133
  219.1 4.3 copy-start.7
  222.3 1.1 copy-start.2
  237.4 81.7 %copy-start.6 = (bf16[1,6144,288]{1,2,0:T(8,128)(2,1)S(1)}, bf16[1,6144,288]{1,2,0:T(8,128)(2,1)}, u32[]{:S(2)}) copy-start(bf16[1,6144,288]{1,2,0:T(8,128)(2,1)} %param.25) | copy-start | bytes 10616836
  316.4 2.7 copy-start.1
  333.9 89.3 %copy-start.5 = (f32[128,2]{0,1:T(2,128)S(1)}, f32[128,2]{0,1:T(2,128)}, u32[]{:S(2)}) copy-start(f32[128,2]{0,1:T(2,128)} %param.24) | copy-start | bytes 3076
  418.9 10.7 %all-to-all-start.3 = ((bf16[4,4,6144]{2,1,0:T(4,128)(2,1)}), bf16[4,4,6144]{2,1,0:T(4,128)(2,1)}, u32[]{:S(2)}, u32[]{:S(2)}) async-start(bf16[4,4,6144]{2,1,0:T(4,128)(2,1)} %reshape.118), calls=%async_computation.4 | async-start | bytes 393216 | tf_op jit(solution)/shard_map/all_to_all | solution.py:140
Sparse Core Ops, SparseCore 0:
  26.9 65.4 all-gather.3
  334.1 83.1 reduce-scatter.1
